TPU v7x, 512 devices: a whole 4x4x16 slice. The times are simulated.
512 devices in a mesh: rows: 32 (over z_lo, y), blk: 16 (over x, z_hi, core).
Axes of the slice: x: 4, y: 4, z: 16 (z_hi: 2, z_lo: 8; z = z_hi * 8 + z_lo), core: 2. Of those that a mesh axis runs over, the one named last changes fastest.
Arguments:
- features: bfloat16 [131072, 1024], P(('rows', 'blk')), may hold values from -6 to 6
- tiles: bfloat16 [512, 7, 256, 256], P(('rows', 'blk')), may hold values from -0.1875 to 0.1875
- tile_cols: int32 [512, 7], P(('rows', 'blk')), may hold values from 0 to 511, as said below
- tile_count: int32 [512], P(('rows', 'blk')), may hold values from 1 to 7
- weight: bfloat16 [1024, 1024], P(('rows', 'blk')), may hold values from -0.1875 to 0.1875
- cotangent: bfloat16 [131072, 1024], P(('rows', 'blk')), may hold values from -0.0625 to 0.0625
Outputs:
- output: bfloat16 [131072, 1024], P(('rows', 'blk'))
- weight_grad: float32 [1024, 1024], P(('rows', 'blk'))
Inputs may be any that keep to these rules, and one draw needn't show every extreme that they name: For each row block g, the first tile_count[g] entries of tile_cols[g] are distinct blocks of g's group of 16 blocks (blocks 16 * (g // 16) onward), each at most 3 positions from g around that group, g itself among them; the later entries are also blocks of that group and carry no tile.
All inputs are finite; a program needn't handle non-finite values.
Results may differ from a plain program's by a relative error of at most 0.0054.
Values may be sent and summed in bfloat16 or wider, within the bound.
A program may use at most 64 MiB of HBM per device.

v0:
```python
import jax
import jax.numpy as jnp
from jax import lax
from jax.sharding import PartitionSpec as P


def passed_along(value, axis, by):
    length = lax.axis_size(axis)
    return lax.ppermute(value, axis, [(i, (i + by) % length) for i in range(length)])


def local(features, tiles, tile_cols, tile_count, weight, cotangent):
    cycle_len = lax.axis_size("blk")
    position = lax.axis_index("blk")
    per_dev = tiles.shape[0]
    slot_total = tiles.shape[1]
    tile_side = tiles.shape[2]
    group_len = cycle_len * per_dev
    slot_ids = jnp.arange(slot_total, dtype=jnp.int32)
    columns = tile_cols % group_len

    def apply_panel(totals, panel_now, source):
        running = totals[0]
        in_use = slot_ids < tile_count[0]
        wanted = source * per_dev + 0
        match = jnp.logical_and(in_use, columns[0] == wanted)
        present = jnp.any(match)
        chosen_slot = jnp.sum(jnp.where(match, slot_ids, 0))
        chosen = lax.dynamic_index_in_dim(tiles[0], chosen_slot, 0, keepdims=False)
        rows_there = panel_now

        def multiply(chosen=chosen, rows_there=rows_there):
            return jnp.dot(chosen, rows_there, preferred_element_type=jnp.float32)

        def nothing():
            return jnp.zeros(running.shape, jnp.float32)

        running = running + lax.cond(present, multiply, nothing)
        updated = [running]
        return tuple(updated)

    empty = jnp.zeros((tile_side, features.shape[1]), jnp.float32)
    totals = tuple((empty for block_here in range(per_dev)))
    totals = apply_panel(totals, features, position)
    reach_blocks = min(3, (group_len - 1) // 2)
    reach_dev = (reach_blocks + per_dev - 1) // per_dev
    from_left = features
    from_right = features
    for offset in range(1, reach_dev + 1):
        from_left = passed_along(from_left, "blk", 1)
        totals = apply_panel(totals, from_left, (position - offset + cycle_len) % cycle_len)
        from_right = passed_along(from_right, "blk", -1)
        totals = apply_panel(totals, from_right, (position + offset) % cycle_len)
    aggregated = totals[0].astype(jnp.bfloat16)
    pre_act = lax.dot_general(
        aggregated,
        lax.all_gather(weight, ("rows", "blk"), axis=0, tiled=True),
        (((1,), (1,)), ((), ())),
        preferred_element_type=jnp.float32,
    )
    output = jax.nn.silu(pre_act).astype(jnp.bfloat16)
    sigmoid_y = jax.nn.sigmoid(pre_act)
    grad_pre = (
        cotangent.astype(jnp.float32) * sigmoid_y * (1.0 + pre_act * (1.0 - sigmoid_y))
    ).astype(jnp.bfloat16)
    weight_grad = lax.psum_scatter(
        lax.dot_general(
            grad_pre, aggregated, (((0,), (0,)), ((), ())), preferred_element_type=jnp.float32
        ),
        ("rows", "blk"),
        scatter_dimension=0,
        tiled=True,
    )
    return (output, weight_grad)


def solution(mesh):
    in_specs = (
        P(("rows", "blk"), None),
        P(("rows", "blk"), None, None, None),
        P(("rows", "blk"), None),
        P(("rows", "blk")),
        P(("rows", "blk"), None),
        P(("rows", "blk"), None),
    )
    out_specs = (P(("rows", "blk"), None), P(("rows", "blk"), None))
    return jax.shard_map(local, mesh=mesh, in_specs=in_specs, out_specs=out_specs, check_vma=False)
```

profile of v0, /device:TPU:2, one launch (start us, length us, event | category | flops | bytes accessed | tf_op | source)
XLA Modules:
  0.0 1387.6 jit_solution(14543954781679902342)
XLA Ops:
  7.9 1.9 collective-permute-start
  9.9 15.1 %collective-permute-start.1 = (bf16[256,1024]{1,0:T(8,128)(2,1)}, bf16[256,1024]{1,0:T(8,128)(2,1)S(1)}, u32[]{:S(2)}, u32[]{:S(2)}) collective-permute-start(bf16[256,1024]{1,0:T(8,128)(2,1)} %param.20), channel_id=1, source_target_pairs={{0,15},{1,0},{2,1},{3,2},{4,3},{5,4},{6,5},{7,6},{8,7},{9,8},{10,9... | collective-permute-start | bytes 1572872 | tf_op jit(solution)/shard_map/ppermute | solution.py:9
  25.0 5.4 collective-permute-done
  31.2 21.4 %collective-permute-start.2 = (bf16[256,1024]{1,0:T(8,128)(2,1)S(1)}, bf16[256,1024]{1,0:T(8,128)(2,1)}, u32[]{:S(2)}, u32[]{:S(2)}) collective-permute-start(bf16[256,1024]{1,0:T(8,128)(2,1)S(1)} %collective-permute-done), channel_id=1, source_target_pairs={{0,1},{1,2},{2,3},{3,4},{4,5},{5,6},{6,7},{7,8},{8,9},{9,10},{10,1... | collective-permute-start | bytes 1572872 | tf_op jit(solution)/shard_map/ppermute | solution.py:9
  52.6 6.6 collective-permute-done.1
  59.2 13.5 collective-permute-start.3
  72.7 6.4 collective-permute-done.2
  79.2 8.0 collective-permute-start.4
  87.7 13.8 collective-permute-start.5
  102.2 1.4 fusion.32
  108.6 3.8 conditional.7
  111.0 1.4 fusion
  112.4 3.9 conditional.9
  115.1 1.2 fusion.8
  116.5 5.0 conditional.10
  119.1 2.4 fusion.12
  123.7 8.2 collective-permute-done.5
  133.1 3.6 add_convert_fusion
  136.7 747.7 %all-gather.3.cloned.1.call-done = bf16[512,2,1024]{2,1,0:T(2,128)(2,1)} async-done(((bf16[1,2,1024]{2,1,0:T(2,128)(2,1)}), bf16[512,2,1024]{2,1,0:T(2,128)(2,1)}) %all-gather.3.cloned.1.call-update) | async-done | bytes 2097168 | tf_op jit(solution)/shard_map/all_gather | solution.py:57
  884.4 2.7 reshape.33
  887.2 1.6 multiply_convert_fusion.1
  888.8 3.0 fusion.28
  891.9 487.5 %all-reduce.3.cloned.1.call-done = f32[1024,1024]{1,0:T(8,128)} async-done(((f32[1024,1024]{1,0:T(8,128)}), f32[1024,1024]{1,0:T(8,128)}) %all-reduce.3.cloned.1.call-update) | async-done | bytes 4194320
  1379.4 1.4 constant_dynamic-slice_fusion
  (31 shorter events, 11.7 us)
Async XLA Ops:
  7.2 877.3 %all-gather.3.cloned.1.call-start = ((), (), s32[]{:S(2)}) async-start(), calls=%async_computation | async-start | bytes 2101248 | tf_op jit(solution)/shard_map/all_gather | solution.py:57
  7.9 1371.5 %all-reduce.3.cloned.1.call-start = ((), (), s32[]{:S(2)}) async-start(), calls=%async_computation.1 | async-start | bytes 8388608
  7.9 22.5 %collective-permute-start = (bf16[256,1024]{1,0:T(8,128)(2,1)}, bf16[256,1024]{1,0:T(8,128)(2,1)S(1)}, u32[]{:S(2)}, u32[]{:S(2)}) collective-permute-start(bf16[256,1024]{1,0:T(8,128)(2,1)} %param.20), channel_id=1, source_target_pairs={{0,1},{1,2},{2,3},{3,4},{4,5},{5,6},{6,7},{7,8},{8,9},{9,10},{10,1... | collective-permute-start | bytes 1572872 | tf_op jit(solution)/shard_map/ppermute | solution.py:9
  9.9 49.4 %collective-permute-start.1 = (bf16[256,1024]{1,0:T(8,128)(2,1)}, bf16[256,1024]{1,0:T(8,128)(2,1)S(1)}, u32[]{:S(2)}, u32[]{:S(2)}) collective-permute-start(bf16[256,1024]{1,0:T(8,128)(2,1)} %param.20), channel_id=1, source_target_pairs={{0,15},{1,0},{2,1},{3,2},{4,3},{5,4},{6,5},{7,6},{8,7},{9,8},{10,9... | collective-permute-start | bytes 1572872 | tf_op jit(solution)/shard_map/ppermute | solution.py:9
  30.4 0.8 copy-start
  31.2 47.9 %collective-permute-start.2 = (bf16[256,1024]{1,0:T(8,128)(2,1)S(1)}, bf16[256,1024]{1,0:T(8,128)(2,1)}, u32[]{:S(2)}, u32[]{:S(2)}) collective-permute-start(bf16[256,1024]{1,0:T(8,128)(2,1)S(1)} %collective-permute-done), channel_id=1, source_target_pairs={{0,1},{1,2},{2,3},{3,4},{4,5},{5,6},{6,7},{7,8},{8,9},{9,10},{10,1... | collective-permute-start | bytes 1572872 | tf_op jit(solution)/shard_map/ppermute | solution.py:9
  59.2 28.4 %collective-permute-start.3 = (bf16[256,1024]{1,0:T(8,128)(2,1)S(1)}, bf16[256,1024]{1,0:T(8,128)(2,1)}, u32[]{:S(2)}, u32[]{:S(2)}) collective-permute-start(bf16[256,1024]{1,0:T(8,128)(2,1)S(1)} %collective-permute-done.1), channel_id=1, source_target_pairs={{0,15},{1,0},{2,1},{3,2},{4,3},{5,4},{6,5},{7,6},{8,7},{9,8},{10,9... | collective-permute-start | bytes 1572872 | tf_op jit(solution)/shard_map/ppermute | solution.py:9
  79.2 43.5 %collective-permute-start.4 = (bf16[256,1024]{1,0:T(8,128)(2,1)}, bf16[256,1024]{1,0:T(8,128)(2,1)}, u32[]{:S(2)}, u32[]{:S(2)}) collective-permute-start(bf16[256,1024]{1,0:T(8,128)(2,1)} %collective-permute-done.2), channel_id=1, source_target_pairs={{0,1},{1,2},{2,3},{3,4},{4,5},{5,6},{6,7},{7,8},{8,9},{9,10},{10,1... | collective-permute-start | bytes 1572872 | tf_op jit(solution)/shard_map/ppermute | solution.py:9
  87.7 44.3 %collective-permute-start.5 = (bf16[256,1024]{1,0:T(8,128)(2,1)}, bf16[256,1024]{1,0:T(8,128)(2,1)}, u32[]{:S(2)}, u32[]{:S(2)}) collective-permute-start(bf16[256,1024]{1,0:T(8,128)(2,1)} %collective-permute-done.3), channel_id=1, source_target_pairs={{0,15},{1,0},{2,1},{3,2},{4,3},{5,4},{6,5},{7,6},{8,7},{9,8},{10,9... | collective-permute-start | bytes 1572872 | tf_op jit(solution)/shard_map/ppermute | solution.py:9
  136.7 750.5 %copy-start.1 = (bf16[256,1024]{1,0:T(8,128)(2,1)S(1)}, bf16[256,1024]{1,0:T(8,128)(2,1)}, u32[]{:S(2)}) copy-start(bf16[256,1024]{1,0:T(8,128)(2,1)} %add_convert_fusion) | copy-start | bytes 1572868
  887.2 1.6 copy-start.2
Sparse Core Ops, SparseCore 0:
  10.1 874.2 all-gather.2
  892.0 487.3 all-reduce.2
where the time goes:
time: 1390 us
  waiting for transfers between devices  1260 us (91%)
  starting transfers between devices  73.8 us (5%)
  between operations  19.2 us (1%)
    all_gather x1, waiting for transfers between devices, local(): lax.all_gather(weight, ('rows', 'blk'), axis=0, tiled=True)  748 us
    unnamed x3, waiting for transfers between devices  488 us
    ppermute x6, starting transfers between devices, passed_along(): lax.ppermute(value, axis, [(i, (i + by) % length) for i in range(length)])  73.7 us
  transfers between devices with their start and end apart: 8, of which 7 were waited for; matrix products, arithmetic and copies ran while one was open for 1% of the time, Pallas kernels for 0%

commit v1 on v0

--- a/solution.py
+++ b/solution.py
@@ -2,6 +2,18 @@
 import jax.numpy as jnp
 from jax import lax
 from jax.sharding import PartitionSpec as P
+
+
+def _put_pairs_all(inp, named_axis):
+    return jnp.concatenate(
+        lax.all_to_all(
+            jnp.stack([inp for _ in range(lax.axis_size(named_axis))], axis=0),
+            concat_axis=0,
+            split_axis=0,
+            axis_name=named_axis,
+        ),
+        axis=0,
+    )
 
 
 def passed_along(value, axis, by):
@@ -54,7 +66,7 @@
     aggregated = totals[0].astype(jnp.bfloat16)
     pre_act = lax.dot_general(
         aggregated,
-        lax.all_gather(weight, ("rows", "blk"), axis=0, tiled=True),
+        _put_pairs_all(weight, ("rows", "blk")),
         (((1,), (1,)), ((), ())),
         preferred_element_type=jnp.float32,
     )

time: 1390 us -> 828 us (0.60)
  waiting for transfers between devices: 1260 us -> 701 us
    all_gather x1 -> x0, waiting for transfers between devices: 748 us -> none  [local(): lax.all_gather(weight, ('rows', 'blk'), axis=0, tiled=True)]
    ppermute x6, waiting for transfers between devices: 27.2 us -> 177 us  [passed_along(): lax.ppermute(value, axis, [(i, (i + by) % length) for i in range(length)])]
    unnamed x3 -> x2, waiting for transfers between devices: 488 us -> 524 us
    ppermute x6, starting transfers between devices: 73.7 us -> 46.1 us  [passed_along(): lax.ppermute(value, axis, [(i, (i + by) % length) for i in range(length)])]
    all_to_all x0 -> x1, starting transfers between devices: none -> 23.3 us  [_put_pairs_all(): lax.all_to_all(jnp.stack([inp for _ in range(lax.axis_size(named_axis))],...]
  transfers between devices with their start and end apart: 8 -> 8, of which waited for: 7 -> 4; matrix products, arithmetic and copies ran while one was open for 1% -> 2% of each run, Pallas kernels for 0% -> 0%
where the time goes in v1:
time: 828 us; the launch traced here: 827 us
  waiting for transfers between devices  701 us (85%)
  starting transfers between devices  69.4 us (8%)
  between operations  19.2 us (2%)
  matrix products  12.5 us (2%)
  local copies, waits for them, and re-layouts  11.2 us (1%)
    unnamed x2, waiting for transfers between devices  524 us
    ppermute x6, waiting for transfers between devices, passed_along(): lax.ppermute(value, axis, [(i, (i + by) % length) for i in range(length)])  177 us
    ppermute x6, starting transfers between devices, passed_along(): lax.ppermute(value, axis, [(i, (i + by) % length) for i in range(length)])  46.1 us
    all_to_all x1, starting transfers between devices, _put_pairs_all(): lax.all_to_all(jnp.stack([inp for _ in range(lax.axis_size(named_axis))],...  23.3 us
  transfers between devices with their start and end apart: 8, of which 4 were waited for; matrix products, arithmetic and copies ran while one was open for 2% of the time, Pallas kernels for 0%

profile of v1, /device:TPU:2, one launch (start us, length us, event | category | flops | bytes accessed | tf_op | source)
XLA Modules:
  0.0 826.9 jit_solution(3725541395019141923)
XLA Ops:
  7.2 3.1 stack.2
  10.3 23.3 %all-to-all-start = ((bf16[512,2,1024]{2,1,0:T(2,128)(2,1)}), bf16[512,2,1024]{2,1,0:T(2,128)(2,1)S(1)}, u32[]{:S(2)}, u32[]{:S(2)}) async-start(bf16[512,2,1024]{2,1,0:T(2,128)(2,1)} %stack.2), calls=%async_computation | async-start | bytes 4194304 | tf_op jit(solution)/shard_map/all_to_all | solution.py:9
  33.7 2.0 collective-permute-start
  35.7 13.7 %collective-permute-start.1 = (bf16[256,1024]{1,0:T(8,128)(2,1)S(1)}, bf16[256,1024]{1,0:T(8,128)(2,1)S(1)}, u32[]{:S(2)}, u32[]{:S(2)}) collective-permute-start(bf16[256,1024]{1,0:T(8,128)(2,1)S(1)} %copy-done), channel_id=1, source_target_pairs={{0,15},{1,0},{2,1},{3,2},{4,3},{5,4},{6,5},{7,6},{8,7},{9,8},{10,9... | collective-permute-start | bytes 1572872 | tf_op jit(solution)/shard_map/ppermute | solution.py:21
  49.4 101.3 %collective-permute-done = bf16[256,1024]{1,0:T(8,128)(2,1)S(1)} collective-permute-done((bf16[256,1024]{1,0:T(8,128)(2,1)S(1)}, bf16[256,1024]{1,0:T(8,128)(2,1)S(1)}, u32[]{:S(2)}, u32[]{:S(2)}) %collective-permute-start) | collective-permute-done | bytes 524320 | tf_op jit(solution)/shard_map/ppermute | solution.py:21
  150.8 1.9 collective-permute-start.2
  152.7 13.3 %collective-permute-start.3 = (bf16[256,1024]{1,0:T(8,128)(2,1)S(1)}, bf16[256,1024]{1,0:T(8,128)(2,1)}, u32[]{:S(2)}, u32[]{:S(2)}) collective-permute-start(bf16[256,1024]{1,0:T(8,128)(2,1)S(1)} %collective-permute-done.1), channel_id=1, source_target_pairs={{0,15},{1,0},{2,1},{3,2},{4,3},{5,4},{6,5},{7,6},{8,7},{9,8},{10,9... | collective-permute-start | bytes 1572872 | tf_op jit(solution)/shard_map/ppermute | solution.py:21
  166.0 59.3 %collective-permute-done.2 = bf16[256,1024]{1,0:T(8,128)(2,1)} collective-permute-done((bf16[256,1024]{1,0:T(8,128)(2,1)S(1)}, bf16[256,1024]{1,0:T(8,128)(2,1)}, u32[]{:S(2)}, u32[]{:S(2)}) %collective-permute-start.2) | collective-permute-done | bytes 524320 | tf_op jit(solution)/shard_map/ppermute | solution.py:21
  225.3 1.9 collective-permute-start.4
  227.2 13.3 %collective-permute-start.5 = (bf16[256,1024]{1,0:T(8,128)(2,1)}, bf16[256,1024]{1,0:T(8,128)(2,1)}, u32[]{:S(2)}, u32[]{:S(2)}) collective-permute-start(bf16[256,1024]{1,0:T(8,128)(2,1)} %collective-permute-done.3), channel_id=1, source_target_pairs={{0,15},{1,0},{2,1},{3,2},{4,3},{5,4},{6,5},{7,6},{8,7},{9,8},{10,9... | collective-permute-start | bytes 1572872 | tf_op jit(solution)/shard_map/ppermute | solution.py:21
  247.0 3.8 conditional.7
  249.4 1.4 fusion
  250.9 4.9 conditional.9
  253.4 2.4 fusion.8
  256.9 5.0 conditional.10
  259.5 2.4 fusion.12
  261.9 1.1 conditional.11
  263.0 16.7 %collective-permute-done.4 = bf16[256,1024]{1,0:T(8,128)(2,1)} collective-permute-done((bf16[256,1024]{1,0:T(8,128)(2,1)}, bf16[256,1024]{1,0:T(8,128)(2,1)}, u32[]{:S(2)}, u32[]{:S(2)}) %collective-permute-start.4) | collective-permute-done | bytes 524320 | tf_op jit(solution)/shard_map/ppermute | solution.py:21
  282.0 4.3 add_convert_fusion
  286.3 2.2 reshape.37
  288.5 3.3 multiply_convert_fusion.1
  291.8 3.0 fusion.28
  294.8 523.9 %all-reduce.3.cloned.1.call-done = f32[1024,1024]{1,0:T(8,128)} async-done(((f32[1024,1024]{1,0:T(8,128)}), f32[1024,1024]{1,0:T(8,128)}) %all-reduce.3.cloned.1.call-update) | async-done | bytes 4194320
  818.7 1.4 constant_dynamic-slice_fusion
  (39 shorter events, 11.4 us)
Async XLA Ops:
  10.3 23.4 %copy-start = (bf16[256,1024]{1,0:T(8,128)(2,1)S(1)}, bf16[256,1024]{1,0:T(8,128)(2,1)}, u32[]{:S(2)}) copy-start(bf16[256,1024]{1,0:T(8,128)(2,1)} %param.20) | copy-start | bytes 1572868
  10.3 230.9 %copy-start.5 = (s32[1,7]{1,0:T(1,128)S(1)}, s32[1,7]{1,0:T(1,128)}, u32[]{:S(2)}) copy-start(s32[1,7]{1,0:T(1,128)} %param.22) | copy-start | bytes 88
  10.3 276.0 %all-to-all-start = ((bf16[512,2,1024]{2,1,0:T(2,128)(2,1)}), bf16[512,2,1024]{2,1,0:T(2,128)(2,1)S(1)}, u32[]{:S(2)}, u32[]{:S(2)}) async-start(bf16[512,2,1024]{2,1,0:T(2,128)(2,1)} %stack.2), calls=%async_computation | async-start | bytes 4194304 | tf_op jit(solution)/shard_map/all_to_all | solution.py:9
  33.6 785.1 %all-reduce.3.cloned.1.call-start = ((), (), s32[]{:S(2)}) async-start(), calls=%async_computation.1 | async-start | bytes 8388608
  33.7 117.1 %collective-permute-start = (bf16[256,1024]{1,0:T(8,128)(2,1)S(1)}, bf16[256,1024]{1,0:T(8,128)(2,1)S(1)}, u32[]{:S(2)}, u32[]{:S(2)}) collective-permute-start(bf16[256,1024]{1,0:T(8,128)(2,1)S(1)} %copy-done), channel_id=1, source_target_pairs={{0,1},{1,2},{2,3},{3,4},{4,5},{5,6},{6,7},{7,8},{8,9},{9,10},{10,1... | collective-permute-start | bytes 1572872 | tf_op jit(solution)/shard_map/ppermute | solution.py:21
  35.7 117.0 %collective-permute-start.1 = (bf16[256,1024]{1,0:T(8,128)(2,1)S(1)}, bf16[256,1024]{1,0:T(8,128)(2,1)S(1)}, u32[]{:S(2)}, u32[]{:S(2)}) collective-permute-start(bf16[256,1024]{1,0:T(8,128)(2,1)S(1)} %copy-done), channel_id=1, source_target_pairs={{0,15},{1,0},{2,1},{3,2},{4,3},{5,4},{6,5},{7,6},{8,7},{9,8},{10,9... | collective-permute-start | bytes 1572872 | tf_op jit(solution)/shard_map/ppermute | solution.py:21
  150.8 96.2 %copy-start.2 = (bf16[256,1024]{1,0:T(8,128)(2,1)}, bf16[256,1024]{1,0:T(8,128)(2,1)S(1)}, u32[]{:S(2)}) copy-start(bf16[256,1024]{1,0:T(8,128)(2,1)S(1)} %collective-permute-done) | copy-start | bytes 1572868
  150.8 74.5 %collective-permute-start.2 = (bf16[256,1024]{1,0:T(8,128)(2,1)S(1)}, bf16[256,1024]{1,0:T(8,128)(2,1)}, u32[]{:S(2)}, u32[]{:S(2)}) collective-permute-start(bf16[256,1024]{1,0:T(8,128)(2,1)S(1)} %collective-permute-done), channel_id=1, source_target_pairs={{0,1},{1,2},{2,3},{3,4},{4,5},{5,6},{6,7},{7,8},{8,9},{9,10},{10,1... | collective-permute-start | bytes 1572872 | tf_op jit(solution)/shard_map/ppermute | solution.py:21
  152.7 72.6 %copy-start.3 = (bf16[256,1024]{1,0:T(8,128)(2,1)}, bf16[256,1024]{1,0:T(8,128)(2,1)S(1)}, u32[]{:S(2)}) copy-start(bf16[256,1024]{1,0:T(8,128)(2,1)S(1)} %collective-permute-done.1) | copy-start | bytes 1572868
  152.7 74.5 %collective-permute-start.3 = (bf16[256,1024]{1,0:T(8,128)(2,1)S(1)}, bf16[256,1024]{1,0:T(8,128)(2,1)}, u32[]{:S(2)}, u32[]{:S(2)}) collective-permute-start(bf16[256,1024]{1,0:T(8,128)(2,1)S(1)} %collective-permute-done.1), channel_id=1, source_target_pairs={{0,15},{1,0},{2,1},{3,2},{4,3},{5,4},{6,5},{7,6},{8,7},{9,8},{10,9... | collective-permute-start | bytes 1572872 | tf_op jit(solution)/shard_map/ppermute | solution.py:21
  225.3 54.5 %collective-permute-start.4 = (bf16[256,1024]{1,0:T(8,128)(2,1)}, bf16[256,1024]{1,0:T(8,128)(2,1)}, u32[]{:S(2)}, u32[]{:S(2)}) collective-permute-start(bf16[256,1024]{1,0:T(8,128)(2,1)} %collective-permute-done.2), channel_id=1, source_target_pairs={{0,1},{1,2},{2,3},{3,4},{4,5},{5,6},{6,7},{7,8},{8,9},{9,10},{10,1... | collective-permute-start | bytes 1572872 | tf_op jit(solution)/shard_map/ppermute | solution.py:21
  227.2 53.7 %collective-permute-start.5 = (bf16[256,1024]{1,0:T(8,128)(2,1)}, bf16[256,1024]{1,0:T(8,128)(2,1)}, u32[]{:S(2)}, u32[]{:S(2)}) collective-permute-start(bf16[256,1024]{1,0:T(8,128)(2,1)} %collective-permute-done.3), channel_id=1, source_target_pairs={{0,15},{1,0},{2,1},{3,2},{4,3},{5,4},{6,5},{7,6},{8,7},{9,8},{10,9... | collective-permute-start | bytes 1572872 | tf_op jit(solution)/shard_map/ppermute | solution.py:21
  247.1 2.4 copy-start.1
  286.3 2.3 copy-start.4
  288.5 3.3 copy-start.6
Sparse Core Ops, SparseCore 0:
  294.9 523.7 all-reduce.2
